TPU v7x, 32 devices: a whole 2x2x4 slice. The times are simulated.
32 devices in a mesh: tm: 8 (over z, x), col: 4 (over y, core).
Axes of the slice: x: 2, y: 2, z: 4, core: 2. Of those that a mesh axis runs over, the one named last changes fastest.
Arguments:
- jacobians: float32 [96, 512, 512], P('tm'), may hold values from -0.05 to 1.05
- increments: float32 [96, 512], P('tm'), may hold values from -1.5 to 1.5
- initial: float32 [512], P('col'), may hold values from -6 to 6
Outputs:
- states: float32 [96, 512], P('tm', 'col')
All inputs are finite; a program needn't handle non-finite values.
Results may differ from a plain program's by a relative error of at most 0.0003.
Values sent between devices are 32-bit elements; how exact they have to be, the bound alone decides.
No kernel may reach another device: no remote copies, remote signals or barrier semaphores. Data moves between devices by JAX's collectives and lax.ppermute only.
A program may use at most 128 MiB of HBM per device.

v0:
```python
import jax
import jax.numpy as jnp
from jax import lax
from jax.sharding import PartitionSpec as P


def from_behind(block, axis, distance):
    devices = range(lax.axis_size(axis))
    route = [(i - distance, i) for i in devices if i - distance in devices]
    return lax.ppermute(block, axis, route)


def matmul(left, right):
    return jnp.dot(left, right, precision=lax.Precision.HIGHEST, preferred_element_type=jnp.float32)


def body(jacobians, increments, initial):
    part_cols = initial.shape[0]
    column_index = lax.axis_index("col")
    segment_index = lax.axis_index("tm")
    rounds = (lax.axis_size("tm") - 1).bit_length()
    first_col = column_index * part_cols

    def own_cols(matrix):
        return lax.dynamic_slice_in_dim(matrix, first_col, part_cols, matrix.ndim - 1)

    def advance_map(running, inputs):
        step_jac, step_inc = inputs
        return ((matmul(step_jac, running[0]), matmul(step_jac, running[1]) + step_inc), None)

    composed, _ = lax.scan(
        advance_map, (own_cols(jacobians[0]), increments[0]), (jacobians[1:], increments[1:])
    )
    acc_map, acc_off = composed
    for level_index in range(rounds):
        distance = 1 << level_index
        recv_map, recv_off = from_behind((acc_map, acc_off), "tm", distance)

        def fold_columns(running, col_block, first_row, recv_map=recv_map, recv_off=recv_off):
            return (matmul(col_block, recv_map), running[1] + matmul(col_block, recv_off))

        new_map, new_off = fold_columns(
            (jnp.zeros_like(acc_map), acc_off),
            lax.all_gather(acc_map, "col", axis=1, tiled=True),
            jnp.int32(0),
        )
        active = segment_index >= distance
        acc_map = jnp.where(active, new_map, acc_map)
        acc_off = jnp.where(active, new_off, acc_off)
    end_part = matmul(acc_map, initial)
    end_mine = lax.psum_scatter(end_part, "col", scatter_dimension=0, tiled=True) + own_cols(
        acc_off
    )
    handed = from_behind(end_mine, "tm", 1)
    start_mine = jnp.where(segment_index == 0, initial, handed)
    start_full = lax.all_gather(start_mine, "col", axis=0, tiled=True)

    def advance_state(current, inputs):
        step_jac, step_inc = inputs
        following = matmul(step_jac, current) + step_inc
        return (following, own_cols(following))

    _, leading = lax.scan(advance_state, start_full, (jacobians[:-1], increments[:-1]))
    return jnp.concatenate([leading, end_mine[None, :]], axis=0)


def solution(mesh):
    return jax.shard_map(
        body,
        mesh=mesh,
        in_specs=(P("tm", None, None), P("tm", None), P("col")),
        out_specs=P("tm", "col"),
        check_vma=False,
    )
```

profile of v0, /device:TPU:25, one launch (start us, length us, event | category | flops | bytes accessed | tf_op | source)
XLA Modules:
  0.0 202.7 jit_solution(5260583161376502509)
XLA Ops:
  6.5 17.6 %fusion.15 = (f32[11,512,512]{2,1,0:T(8,128)}, f32[11,512,512]{2,1,0:T(8,128)}) fusion(f32[12,512,512]{2,1,0:T(8,128)} %param.7), kind=kLoop, calls=%fused_computation.28 | loop fusion | bytes 46137344 | tf_op jit(solution)/shard_map/slice | solution.py:63
  24.2 49.5 %while.26 = (s32[]{:T(128)}, f32[512,128]{1,0:T(8,128)S(1)}, f32[512]{0:T(512)S(1)}, f32[11,512,512]{2,1,0:T(8,128)}, f32[11,512]{1,0:T(8,128)S(1)}, /*index=5*/s32[]{:T(128)}) while((s32[]{:T(128)}, f32[512,128]{1,0:T(8,128)S(1)}, f32[512]{0:T(512)S(1)}, f32[11,512,512]{2,1,0:T(8,128)}, f32[11,512]{1,0:T(8,128)S(1)}, ...), condition=%wide.region_1.2_spmd, body=%wide.region_0.1_spmd.sunk | while | flops 405799424 | bytes 3161161 | solution.py:31
  26.5 2.2 %fusion.49 = f32[512,128]{1,0:T(8,128)S(1)} fusion(f32[512,128]{1,0:T(8,128)S(1)} %copy.24, f32[11,512,512]{2,1,0:T(8,128)} %get-tuple-element.219, s32[]{:T(128)} %get-tuple-element.210), kind=kOutput, calls=%fused_computation.2.clone.1 | convolution fusion | flops 402653184 | bytes 1573376 | tf_op jit(solution)/shard_map/while/body/eval_jaxpr/dot_general | solution.py:14
  31.0 2.2 %fusion.49 = f32[512,128]{1,0:T(8,128)S(1)} fusion(f32[512,128]{1,0:T(8,128)S(1)} %copy.24, f32[11,512,512]{2,1,0:T(8,128)} %get-tuple-element.219, s32[]{:T(128)} %get-tuple-element.210), kind=kOutput, calls=%fused_computation.2.clone.1 | convolution fusion | flops 402653184 | bytes 1573376 | tf_op jit(solution)/shard_map/while/body/eval_jaxpr/dot_general | solution.py:14
  35.5 2.2 %fusion.49 = f32[512,128]{1,0:T(8,128)S(1)} fusion(f32[512,128]{1,0:T(8,128)S(1)} %copy.24, f32[11,512,512]{2,1,0:T(8,128)} %get-tuple-element.219, s32[]{:T(128)} %get-tuple-element.210), kind=kOutput, calls=%fused_computation.2.clone.1 | convolution fusion | flops 402653184 | bytes 1573376 | tf_op jit(solution)/shard_map/while/body/eval_jaxpr/dot_general | solution.py:14
  40.0 2.2 %fusion.49 = f32[512,128]{1,0:T(8,128)S(1)} fusion(f32[512,128]{1,0:T(8,128)S(1)} %copy.24, f32[11,512,512]{2,1,0:T(8,128)} %get-tuple-element.219, s32[]{:T(128)} %get-tuple-element.210), kind=kOutput, calls=%fused_computation.2.clone.1 | convolution fusion | flops 402653184 | bytes 1573376 | tf_op jit(solution)/shard_map/while/body/eval_jaxpr/dot_general | solution.py:14
  44.5 2.2 %fusion.49 = f32[512,128]{1,0:T(8,128)S(1)} fusion(f32[512,128]{1,0:T(8,128)S(1)} %copy.24, f32[11,512,512]{2,1,0:T(8,128)} %get-tuple-element.219, s32[]{:T(128)} %get-tuple-element.210), kind=kOutput, calls=%fused_computation.2.clone.1 | convolution fusion | flops 402653184 | bytes 1573376 | tf_op jit(solution)/shard_map/while/body/eval_jaxpr/dot_general | solution.py:14
  49.0 2.2 %fusion.49 = f32[512,128]{1,0:T(8,128)S(1)} fusion(f32[512,128]{1,0:T(8,128)S(1)} %copy.24, f32[11,512,512]{2,1,0:T(8,128)} %get-tuple-element.219, s32[]{:T(128)} %get-tuple-element.210), kind=kOutput, calls=%fused_computation.2.clone.1 | convolution fusion | flops 402653184 | bytes 1573376 | tf_op jit(solution)/shard_map/while/body/eval_jaxpr/dot_general | solution.py:14
  53.5 2.2 %fusion.49 = f32[512,128]{1,0:T(8,128)S(1)} fusion(f32[512,128]{1,0:T(8,128)S(1)} %copy.24, f32[11,512,512]{2,1,0:T(8,128)} %get-tuple-element.219, s32[]{:T(128)} %get-tuple-element.210), kind=kOutput, calls=%fused_computation.2.clone.1 | convolution fusion | flops 402653184 | bytes 1573376 | tf_op jit(solution)/shard_map/while/body/eval_jaxpr/dot_general | solution.py:14
  58.0 2.2 %fusion.49 = f32[512,128]{1,0:T(8,128)S(1)} fusion(f32[512,128]{1,0:T(8,128)S(1)} %copy.24, f32[11,512,512]{2,1,0:T(8,128)} %get-tuple-element.219, s32[]{:T(128)} %get-tuple-element.210), kind=kOutput, calls=%fused_computation.2.clone.1 | convolution fusion | flops 402653184 | bytes 1573376 | tf_op jit(solution)/shard_map/while/body/eval_jaxpr/dot_general | solution.py:14
  62.5 2.2 %fusion.49 = f32[512,128]{1,0:T(8,128)S(1)} fusion(f32[512,128]{1,0:T(8,128)S(1)} %copy.24, f32[11,512,512]{2,1,0:T(8,128)} %get-tuple-element.219, s32[]{:T(128)} %get-tuple-element.210), kind=kOutput, calls=%fused_computation.2.clone.1 | convolution fusion | flops 402653184 | bytes 1573376 | tf_op jit(solution)/shard_map/while/body/eval_jaxpr/dot_general | solution.py:14
  67.0 2.2 %fusion.49 = f32[512,128]{1,0:T(8,128)S(1)} fusion(f32[512,128]{1,0:T(8,128)S(1)} %copy.24, f32[11,512,512]{2,1,0:T(8,128)} %get-tuple-element.219, s32[]{:T(128)} %get-tuple-element.210), kind=kOutput, calls=%fused_computation.2.clone.1 | convolution fusion | flops 402653184 | bytes 1573376 | tf_op jit(solution)/shard_map/while/body/eval_jaxpr/dot_general | solution.py:14
  71.5 2.2 %fusion.49 = f32[512,128]{1,0:T(8,128)S(1)} fusion(f32[512,128]{1,0:T(8,128)S(1)} %copy.24, f32[11,512,512]{2,1,0:T(8,128)} %get-tuple-element.219, s32[]{:T(128)} %get-tuple-element.210), kind=kOutput, calls=%fused_computation.2.clone.1 | convolution fusion | flops 402653184 | bytes 1573376 | tf_op jit(solution)/shard_map/while/body/eval_jaxpr/dot_general | solution.py:14
  74.5 3.1 %collective-permute-start = (f32[512,128]{1,0:T(8,128)}, f32[512,128]{1,0:T(8,128)S(1)}, u32[]{:S(2)}, u32[]{:S(2)}) collective-permute-start(f32[512,128]{1,0:T(8,128)} %copy-done), channel_id=1, source_target_pairs={{0,4},{4,8},{8,12},{12,16},{16,20},{20,24},{24,28},{1,5},{5,9},{9,... | collective-permute-start | bytes 786440 | tf_op jit(solution)/shard_map/ppermute | solution.py:10
  77.7 7.1 %collective-permute-done = f32[512,128]{1,0:T(8,128)S(1)} collective-permute-done((f32[512,128]{1,0:T(8,128)}, f32[512,128]{1,0:T(8,128)S(1)}, u32[]{:S(2)}, u32[]{:S(2)}) %collective-permute-start) | collective-permute-done | bytes 262176 | tf_op jit(solution)/shard_map/ppermute | solution.py:10
  84.7 8.1 %all-gather.5.cloned.1.call-done = f32[512,512]{1,0:T(8,128)} async-done(((f32[512,128]{1,0:T(8,128)}), f32[512,512]{1,0:T(8,128)}) %all-gather.5.cloned.1.call-update) | async-done | bytes 1048592 | tf_op jit(solution)/shard_map/all_gather | solution.py:44
  92.8 2.9 %convolution_select_fusion.2 = f32[512,128]{1,0:T(8,128)} fusion(f32[512,128]{1,0:T(8,128)} %copy-done, f32[512,512]{1,0:T(8,128)} %all-gather.5.cloned.1.call-done, f32[512,128]{1,0:T(8,128)S(1)} %collective-permute-done, pred[]{:T(512)S(6)} %ge.11), kind=kOutput, calls=%fused_computation.17 | convolution fusion | flops 402718720 | bytes 1835009 | tf_op jit(solution)/shard_map/dot_general | solution.py:14
  97.1 8.4 %collective-permute-done.1 = f32[512,128]{1,0:T(8,128)S(1)} collective-permute-done((f32[512,128]{1,0:T(8,128)}, f32[512,128]{1,0:T(8,128)S(1)}, u32[]{:S(2)}, u32[]{:S(2)}) %collective-permute-start.1) | collective-permute-done | bytes 262176 | tf_op jit(solution)/shard_map/ppermute | solution.py:10
  105.5 7.2 %all-gather.7.cloned.1.call-done = f32[512,512]{1,0:T(8,128)} async-done(((f32[512,128]{1,0:T(8,128)}), f32[512,512]{1,0:T(8,128)}) %all-gather.7.cloned.1.call-update) | async-done | bytes 1048592 | tf_op jit(solution)/shard_map/all_gather | solution.py:44
  112.7 2.9 %convolution_select_fusion.1 = f32[512,128]{1,0:T(8,128)} fusion(f32[512,128]{1,0:T(8,128)} %convolution_select_fusion.2, f32[512,512]{1,0:T(8,128)} %all-gather.7.cloned.1.call-done, f32[512,128]{1,0:T(8,128)S(1)} %collective-permute-done.1, pred[]{:T(512)S(6)} %ge.10), kind=kOutput, calls=%fused_computation.16 | convolution fusion | flops 402718720 | bytes 1835009 | tf_op jit(solution)/shard_map/dot_general | solution.py:14
  115.7 3.1 %collective-permute-start.3 = (f32[512]{0:T(512)S(1)}, f32[512]{0:T(512)S(1)}, u32[]{:S(2)}, u32[]{:S(2)}) collective-permute-start(f32[512]{0:T(512)S(1)} %get-tuple-element.108), channel_id=1, source_target_pairs={{0,4},{4,8},{8,12},{12,16},{16,20},{20,24},{24,28},{1,5},{5,9},{9,... | collective-permute-start | bytes 6152 | tf_op jit(solution)/shard_map/ppermute | solution.py:10
  120.9 2.2 %fusion.17 = f32[1,512]{1,0:T(1,128)S(1)} fusion(f32[512,512]{1,0:T(8,128)} %all-gather.5.cloned.1.call-done, f32[512,1]{0,1:T(1,128)S(1)} %bitcast.89), kind=kOutput, calls=%fused_computation.30 | convolution fusion | flops 3145728 | bytes 1052672 | tf_op jit(solution)/shard_map/dot_general | solution.py:14
  124.5 3.4 %collective-permute-done.4 = f32[512]{0:T(512)S(1)} collective-permute-done((f32[512]{0:T(512)S(1)}, f32[512]{0:T(512)S(1)}, u32[]{:S(2)}, u32[]{:S(2)}) %collective-permute-start.4) | collective-permute-done | bytes 2080 | tf_op jit(solution)/shard_map/ppermute | solution.py:10
  127.9 2.3 %fusion.18 = f32[1,512]{1,0:T(1,128)S(1)} fusion(f32[512,512]{1,0:T(8,128)} %all-gather.7.cloned.1.call-done, f32[512,1]{0,1:T(1,128)S(1)} %bitcast.90), kind=kOutput, calls=%fused_computation.31 | convolution fusion | flops 3145728 | bytes 1052672 | tf_op jit(solution)/shard_map/dot_general | solution.py:14
  137.6 11.9 %collective-permute-done.2 = f32[512,128]{1,0:T(8,128)S(1)} collective-permute-done((f32[512,128]{1,0:T(8,128)}, f32[512,128]{1,0:T(8,128)S(1)}, u32[]{:S(2)}, u32[]{:S(2)}) %collective-permute-start.2) | collective-permute-done | bytes 262176 | tf_op jit(solution)/shard_map/ppermute | solution.py:10
  149.5 2.2 %convolution_select_fusion = f32[512,128]{1,0:T(8,128)S(1)} fusion(f32[512,128]{1,0:T(8,128)} %convolution_select_fusion.1, f32[512,512]{1,0:T(8,128)} %all-gather.9.cloned.1.call-done, f32[512,128]{1,0:T(8,128)S(1)} %collective-permute-done.2, pred[]{:T(512)S(6)} %ge.9), kind=kOutput, calls=%fused_computation.15 | convolution fusion | flops 402718720 | bytes 1835009 | tf_op jit(solution)/shard_map/dot_general | solution.py:14
  152.1 5.5 %all-reduce = f32[512]{0:T(512)S(1)} all-reduce(f32[512]{0:T(512)S(1)} %bitcast.87), channel_id=2, replica_groups=mesh['tm'=8,'col'=4] {'col'}, use_global_device_ids=true, to_apply=%region_2.3.clone | all-reduce | flops 512 | bytes 4096
  159.8 3.1 %collective-permute-done.6 = f32[128]{0:T(128)S(1)} collective-permute-done((f32[128]{0:T(128)S(1)}, f32[128]{0:T(128)S(1)}, u32[]{:S(2)}, u32[]{:S(2)}) %collective-permute-start.6) | collective-permute-done | bytes 544 | tf_op jit(solution)/shard_map/ppermute | solution.py:10
  162.9 6.9 %all-gather = f32[4,1,128]{2,1,0:T(1,128)S(1)} all-gather(f32[1,1,128]{2,1,0:T(1,128)S(1)} %fusion.12), channel_id=1, replica_groups=mesh['tm'=8,'col'=4] {'col'}, dimensions={0}, use_global_device_ids=true | all-gather | bytes 2560 | tf_op jit(solution)/shard_map/all_gather | solution.py:56
  169.8 25.8 %while.27 = (s32[]{:T(128)}, f32[512]{0:T(512)S(1)}, f32[11,128]{1,0:T(8,128)S(1)}, f32[11,512,512]{2,1,0:T(8,128)}, f32[11,512]{1,0:T(8,128)S(1)}, /*index=5*/s32[]{:T(128)}, s32[]{:T(128)}, s32[]{:T(128)}) while((s32[]{:T(128)}, f32[512]{0:T(512)S(1)}, f32[11,128]{1,0:T(8,128)S(1)}, f32[11,512,512]{2,1,0:T(8,128)}, f32[11,512]{1,0:T(8,128)S(1)}, ...), condition=%wide.region_4.5_spmd, body=%wide.region_3.4_spmd.sunk | while | flops 3146242 | bytes 1065569 | solution.py:63
  172.1 2.2 %fusion.53 = f32[1,512]{1,0:T(1,128)S(1)} fusion(f32[512,1]{0,1:T(1,128)S(1)} %bitcast.83, f32[11,512,512]{2,1,0:T(8,128)} %get-tuple-element.241, s32[]{:T(128)} %get-tuple-element.230), kind=kOutput, calls=%fused_computation.9.clone.1 | convolution fusion | flops 3145728 | bytes 1053184 | tf_op jit(solution)/shard_map/while/body/eval_jaxpr/dot_general | solution.py:14
  174.5 2.2 %fusion.53 = f32[1,512]{1,0:T(1,128)S(1)} fusion(f32[512,1]{0,1:T(1,128)S(1)} %bitcast.83, f32[11,512,512]{2,1,0:T(8,128)} %get-tuple-element.241, s32[]{:T(128)} %get-tuple-element.230), kind=kOutput, calls=%fused_computation.9.clone.1 | convolution fusion | flops 3145728 | bytes 1053184 | tf_op jit(solution)/shard_map/while/body/eval_jaxpr/dot_general | solution.py:14
  (135 shorter events, 61.4 us)
Async XLA Ops:
  6.5 86.3 %all-gather.5.cloned.1.call-start = ((), (), s32[]{:S(2)}) async-start(), calls=%async_computation | async-start | bytes 1310720 | tf_op jit(solution)/shard_map/all_gather | solution.py:44
  6.5 17.6 %copy-start.1 = (f32[12,512]{1,0:T(8,128)S(1)}, f32[12,512]{1,0:T(8,128)}, u32[]{:S(2)}) copy-start(f32[12,512]{1,0:T(8,128)} %param.8) | copy-start | bytes 73732
  6.5 17.6 %slice-start = ((f32[12,512,512]{2,1,0:T(8,128)}), f32[1,512,512]{2,1,0:T(8,128)S(1)}, s32[]{:S(2)}) async-start(f32[12,512,512]{2,1,0:T(8,128)} %param.7), calls=%async_computation.3 | async-start | bytes 2097152 | tf_op jit(solution)/shard_map/slice | solution.py:32
  6.5 17.7 %slice-start.1 = ((f32[12,512]{1,0:T(8,128)}), f32[1,512]{1,0:T(1,128)S(1)}, s32[]{:S(2)}) async-start(f32[12,512]{1,0:T(8,128)} %param.8), calls=%async_computation.4 | async-start | bytes 4096 | tf_op jit(solution)/shard_map/slice | solution.py:32
  24.1 107.3 %copy-start.3 = (u32[32]{0:T(128)S(1)}, u32[32]{0:T(128)}, u32[]{:S(2)}) copy-start(u32[32]{0:T(128)} %constant.58) | copy-start | bytes 388
  24.2 127.5 %copy-start.2 = (f32[128]{0:T(128)S(1)}, f32[128]{0:T(128)}, u32[]{:S(2)}) copy-start(f32[128]{0:T(128)} %param.9) | copy-start | bytes 1540
  73.7 0.7 copy-start
  74.5 38.3 %all-gather.7.cloned.1.call-start = ((), (), s32[]{:S(2)}) async-start(), calls=%async_computation.1 | async-start | bytes 1310720 | tf_op jit(solution)/shard_map/all_gather | solution.py:44
  74.5 10.2 %collective-permute-start = (f32[512,128]{1,0:T(8,128)}, f32[512,128]{1,0:T(8,128)S(1)}, u32[]{:S(2)}, u32[]{:S(2)}) collective-permute-start(f32[512,128]{1,0:T(8,128)} %copy-done), channel_id=1, source_target_pairs={{0,4},{4,8},{8,12},{12,16},{16,20},{20,24},{24,28},{1,5},{5,9},{9,... | collective-permute-start | bytes 786440 | tf_op jit(solution)/shard_map/ppermute | solution.py:10
  95.8 39.6 %all-gather.9.cloned.1.call-start = ((), (), s32[]{:S(2)}) async-start(), calls=%async_computation.2 | async-start | bytes 1310720 | tf_op jit(solution)/shard_map/all_gather | solution.py:44
  95.8 9.7 %collective-permute-start.1 = (f32[512,128]{1,0:T(8,128)}, f32[512,128]{1,0:T(8,128)S(1)}, u32[]{:S(2)}, u32[]{:S(2)}) collective-permute-start(f32[512,128]{1,0:T(8,128)} %convolution_select_fusion.2), channel_id=1, source_target_pairs={{0,8},{4,12},{8,16},{12,20},{16,24},{20,28},{1,9},{5,13},{9,17},{1... | collective-permute-start | bytes 786440 | tf_op jit(solution)/shard_map/ppermute | solution.py:10
  115.7 5.2 %collective-permute-start.3 = (f32[512]{0:T(512)S(1)}, f32[512]{0:T(512)S(1)}, u32[]{:S(2)}, u32[]{:S(2)}) collective-permute-start(f32[512]{0:T(512)S(1)} %get-tuple-element.108), channel_id=1, source_target_pairs={{0,4},{4,8},{8,12},{12,16},{16,20},{20,24},{24,28},{1,5},{5,9},{9,... | collective-permute-start | bytes 6152 | tf_op jit(solution)/shard_map/ppermute | solution.py:10
  123.2 4.7 %collective-permute-start.4 = (f32[512]{0:T(512)S(1)}, f32[512]{0:T(512)S(1)}, u32[]{:S(2)}, u32[]{:S(2)}) collective-permute-start(f32[512]{0:T(512)S(1)} %add_select_fusion.2), channel_id=1, source_target_pairs={{0,8},{4,12},{8,16},{12,20},{16,24},{20,28},{1,9},{5,13},{9,17},{1... | collective-permute-start | bytes 6152 | tf_op jit(solution)/shard_map/ppermute | solution.py:10
  130.2 5.2 %collective-permute-start.5 = (f32[512]{0:T(512)S(1)}, f32[512]{0:T(512)S(1)}, u32[]{:S(2)}, u32[]{:S(2)}) collective-permute-start(f32[512]{0:T(512)S(1)} %add_select_fusion.1), channel_id=1, source_target_pairs={{0,16},{4,20},{8,24},{12,28},{1,17},{5,21},{9,25},{13,29},{2,18},{... | collective-permute-start | bytes 6152 | tf_op jit(solution)/shard_map/ppermute | solution.py:10
  132.7 16.8 %collective-permute-start.2 = (f32[512,128]{1,0:T(8,128)}, f32[512,128]{1,0:T(8,128)S(1)}, u32[]{:S(2)}, u32[]{:S(2)}) collective-permute-start(f32[512,128]{1,0:T(8,128)} %convolution_select_fusion.1), channel_id=1, source_target_pairs={{0,16},{4,20},{8,24},{12,28},{1,17},{5,21},{9,25},{13,29},{2,18},{... | collective-permute-start | bytes 786440 | tf_op jit(solution)/shard_map/ppermute | solution.py:10
  157.7 5.2 %collective-permute-start.6 = (f32[128]{0:T(128)S(1)}, f32[128]{0:T(128)S(1)}, u32[]{:S(2)}, u32[]{:S(2)}) collective-permute-start(f32[128]{0:T(128)S(1)} %dynamic-slice_add_fusion), channel_id=1, source_target_pairs={{0,4},{4,8},{8,12},{12,16},{16,20},{20,24},{24,28},{1,5},{5,9},{9,... | collective-permute-start | bytes 1544 | tf_op jit(solution)/shard_map/ppermute | solution.py:10
Sparse Core Ops, SparseCore 0:
  74.6 18.1 all-gather.4
  95.9 16.8 all-gather.6
  115.8 16.8 all-gather.8
where the time goes:
time: 205 us; the launch traced here: 203 us
  matrix products  87.8 us (43%)
  waiting for transfers between devices  52.8 us (26%)
  local copies, waits for them, and re-layouts  20.7 us (10%)
  between operations  14 us (7%)
  starting transfers between devices  13.6 us (7%)
  blocking collectives  12.4 us (6%)
    dot_general x40, matrix products, matmul(): jnp.dot(left, right, precision=lax.Precision.HIGHEST, preferred_element_t...  87.8 us
    ppermute x7, waiting for transfers between devices, from_behind(): return lax.ppermute(block, axis, route)  37.4 us
    slice x1, local copies, waits for them, and re-layouts, body(): jacobians[:-1]  17.6 us
    all_gather x3, waiting for transfers between devices, body(): lax.all_gather(acc_map, 'col', axis=1, tiled=True)  15.3 us
    ppermute x7, starting transfers between devices, from_behind(): return lax.ppermute(block, axis, route)  13.5 us
    all_gather x1, blocking collectives, body(): start_full = lax.all_gather(start_mine, 'col', axis=0, tiled=True)  6.9 us
    unnamed x1, blocking collectives  5.5 us
  transfers between devices with their start and end apart: 10, of which 9 were waited for; matrix products, arithmetic and copies ran while one was open for 4% of the time, Pallas kernels for 0%

commit v1 on v0

--- a/solution.py
+++ b/solution.py
@@ -2,6 +2,17 @@
 import jax.numpy as jnp
 from jax import lax
 from jax.sharding import PartitionSpec as P
+
+
+def gather_around(shard, axis, dim):
+    ways = lax.axis_size(axis)
+    pieces = [shard]
+    for far in range(1, ways):
+        pieces.append(
+            lax.ppermute(pieces[far - 1], axis, [(d, (d - 1) % ways) for d in range(ways)])
+        )
+    line = jnp.concatenate(pieces, axis=dim)
+    return jnp.roll(line, lax.axis_index(axis) * shard.shape[dim], axis=dim)
 
 
 def from_behind(block, axis, distance):
@@ -40,9 +51,7 @@
             return (matmul(col_block, recv_map), running[1] + matmul(col_block, recv_off))
 
         new_map, new_off = fold_columns(
-            (jnp.zeros_like(acc_map), acc_off),
-            lax.all_gather(acc_map, "col", axis=1, tiled=True),
-            jnp.int32(0),
+            (jnp.zeros_like(acc_map), acc_off), gather_around(acc_map, "col", 1), jnp.int32(0)
         )
         active = segment_index >= distance
         acc_map = jnp.where(active, new_map, acc_map)

time: 205 us -> 187 us (0.912)
  between operations: 14 us -> 0.93 us
  matrix products: 87.8 us -> 77.9 us
  starting transfers between devices: 13.6 us -> 18.7 us
  waiting for transfers between devices: 52.8 us -> 48.5 us
  other arithmetic: 0.83 us -> 4.42 us
    ppermute x0 -> x9, waiting for transfers between devices: none -> 34 us  [gather_around(): lax.ppermute(pieces[far - 1], axis, [(d, (d - 1) % ways) for d in range(w...]
    ppermute x7, waiting for transfers between devices: 37.4 us -> 14.6 us  [from_behind(): return lax.ppermute(block, axis, route)]
    all_gather x3 -> x0, waiting for transfers between devices: 15.3 us -> none  [body(): lax.all_gather(acc_map, 'col', axis=1, tiled=True)]
    dot_general x40, matrix products: 87.8 us -> 77.9 us  [matmul(): jnp.dot(left, right, precision=lax.Precision.HIGHEST, preferred_element_t...]
    ppermute x0 -> x9, starting transfers between devices: none -> 6.08 us  [gather_around(): lax.ppermute(pieces[far - 1], axis, [(d, (d - 1) % ways) for d in range(w...]
    concatenate x0 -> x3, other arithmetic: none -> 3.61 us  [gather_around(): return jnp.roll(line, lax.axis_index(axis) * shard.shape[dim], axis=dim)]
  transfers between devices with their start and end apart: 10 -> 16, of which waited for: 9 -> 13; matrix products, arithmetic and copies ran while one was open for 4% -> 4% of each run, Pallas kernels for 0% -> 0%
where the time goes in v1:
time: 187 us; the launch traced here: 185 us
  matrix products  77.9 us (42%)
  waiting for transfers between devices  48.5 us (26%)
  local copies, waits for them, and re-layouts  20.1 us (11%)
  starting transfers between devices  18.7 us (10%)
  blocking collectives  14 us (7%)
  other arithmetic  4.42 us (2%)
    dot_general x40, matrix products, matmul(): jnp.dot(left, right, precision=lax.Precision.HIGHEST, preferred_element_t...  77.9 us
    ppermute x9, waiting for transfers between devices, gather_around(): lax.ppermute(pieces[far - 1], axis, [(d, (d - 1) % ways) for d in range(w...  34 us
    slice x1, local copies, waits for them, and re-layouts, body(): jacobians[:-1]  17.6 us
    ppermute x7, waiting for transfers between devices, from_behind(): return lax.ppermute(block, axis, route)  14.6 us
    ppermute x7, starting transfers between devices, from_behind(): return lax.ppermute(block, axis, route)  12.6 us
    unnamed x1, blocking collectives  7.03 us
    all_gather x1, blocking collectives, body(): start_full = lax.all_gather(start_mine, 'col', axis=0, tiled=True)  6.99 us
    ppermute x9, starting transfers between devices, gather_around(): lax.ppermute(pieces[far - 1], axis, [(d, (d - 1) % ways) for d in range(w...  6.08 us
  transfers between devices with their start and end apart: 16, of which 13 were waited for; matrix products, arithmetic and copies ran while one was open for 4% of the time, Pallas kernels for 0%

profile of v1, /device:TPU:25, one launch (start us, length us, event | category | flops | bytes accessed | tf_op | source)
XLA Modules:
  0.0 185.3 jit_solution(10386349933675849329)
XLA Ops:
  0.0 17.6 %fusion.36 = (f32[11,512,512]{2,1,0:T(8,128)}, f32[11,512,512]{2,1,0:T(8,128)}) fusion(f32[12,512,512]{2,1,0:T(8,128)} %param.9), kind=kLoop, calls=%fused_computation.73 | loop fusion | bytes 46137344 | tf_op jit(solution)/shard_map/slice | solution.py:72
  17.7 49.5 %while.26 = (s32[]{:T(128)}, f32[512,128]{1,0:T(8,128)S(1)}, f32[512]{0:T(512)S(1)}, f32[11,512,512]{2,1,0:T(8,128)}, f32[11,512]{1,0:T(8,128)S(1)}, /*index=5*/s32[]{:T(128)}) while((s32[]{:T(128)}, f32[512,128]{1,0:T(8,128)S(1)}, f32[512]{0:T(512)S(1)}, f32[11,512,512]{2,1,0:T(8,128)}, f32[11,512]{1,0:T(8,128)S(1)}, ...), condition=%wide.region_1.2_spmd, body=%wide.region_0.1_spmd.sunk | while | flops 405799424 | bytes 3161161 | solution.py:42
  17.7 2.2 %fusion.71 = f32[1,512]{1,0:T(1,128)S(1)} fusion(f32[512,1]{0,1:T(1,128)S(1)} %bitcast.80, f32[11,512,512]{2,1,0:T(8,128)} %get-tuple-element.220, s32[]{:T(128)} %get-tuple-element.211), kind=kOutput, calls=%fused_computation.clone.1 | convolution fusion | flops 3145728 | bytes 1053184 | tf_op jit(solution)/shard_map/while/body/eval_jaxpr/dot_general | solution.py:25
  19.9 2.2 %fusion.70 = f32[512,128]{1,0:T(8,128)S(1)} fusion(f32[512,128]{1,0:T(8,128)S(1)} %copy.26, f32[11,512,512]{2,1,0:T(8,128)} %get-tuple-element.220, s32[]{:T(128)} %get-tuple-element.211), kind=kOutput, calls=%fused_computation.2.clone.1 | convolution fusion | flops 402653184 | bytes 1573376 | tf_op jit(solution)/shard_map/while/body/eval_jaxpr/dot_general | solution.py:25
  22.2 2.2 %fusion.71 = f32[1,512]{1,0:T(1,128)S(1)} fusion(f32[512,1]{0,1:T(1,128)S(1)} %bitcast.80, f32[11,512,512]{2,1,0:T(8,128)} %get-tuple-element.220, s32[]{:T(128)} %get-tuple-element.211), kind=kOutput, calls=%fused_computation.clone.1 | convolution fusion | flops 3145728 | bytes 1053184 | tf_op jit(solution)/shard_map/while/body/eval_jaxpr/dot_general | solution.py:25
  24.5 2.2 %fusion.70 = f32[512,128]{1,0:T(8,128)S(1)} fusion(f32[512,128]{1,0:T(8,128)S(1)} %copy.26, f32[11,512,512]{2,1,0:T(8,128)} %get-tuple-element.220, s32[]{:T(128)} %get-tuple-element.211), kind=kOutput, calls=%fused_computation.2.clone.1 | convolution fusion | flops 402653184 | bytes 1573376 | tf_op jit(solution)/shard_map/while/body/eval_jaxpr/dot_general | solution.py:25
  26.7 2.2 %fusion.71 = f32[1,512]{1,0:T(1,128)S(1)} fusion(f32[512,1]{0,1:T(1,128)S(1)} %bitcast.80, f32[11,512,512]{2,1,0:T(8,128)} %get-tuple-element.220, s32[]{:T(128)} %get-tuple-element.211), kind=kOutput, calls=%fused_computation.clone.1 | convolution fusion | flops 3145728 | bytes 1053184 | tf_op jit(solution)/shard_map/while/body/eval_jaxpr/dot_general | solution.py:25
  29.0 2.2 %fusion.70 = f32[512,128]{1,0:T(8,128)S(1)} fusion(f32[512,128]{1,0:T(8,128)S(1)} %copy.26, f32[11,512,512]{2,1,0:T(8,128)} %get-tuple-element.220, s32[]{:T(128)} %get-tuple-element.211), kind=kOutput, calls=%fused_computation.2.clone.1 | convolution fusion | flops 402653184 | bytes 1573376 | tf_op jit(solution)/shard_map/while/body/eval_jaxpr/dot_general | solution.py:25
  33.5 2.2 %fusion.70 = f32[512,128]{1,0:T(8,128)S(1)} fusion(f32[512,128]{1,0:T(8,128)S(1)} %copy.26, f32[11,512,512]{2,1,0:T(8,128)} %get-tuple-element.220, s32[]{:T(128)} %get-tuple-element.211), kind=kOutput, calls=%fused_computation.2.clone.1 | convolution fusion | flops 402653184 | bytes 1573376 | tf_op jit(solution)/shard_map/while/body/eval_jaxpr/dot_general | solution.py:25
  38.0 2.2 %fusion.70 = f32[512,128]{1,0:T(8,128)S(1)} fusion(f32[512,128]{1,0:T(8,128)S(1)} %copy.26, f32[11,512,512]{2,1,0:T(8,128)} %get-tuple-element.220, s32[]{:T(128)} %get-tuple-element.211), kind=kOutput, calls=%fused_computation.2.clone.1 | convolution fusion | flops 402653184 | bytes 1573376 | tf_op jit(solution)/shard_map/while/body/eval_jaxpr/dot_general | solution.py:25
  42.5 2.2 %fusion.70 = f32[512,128]{1,0:T(8,128)S(1)} fusion(f32[512,128]{1,0:T(8,128)S(1)} %copy.26, f32[11,512,512]{2,1,0:T(8,128)} %get-tuple-element.220, s32[]{:T(128)} %get-tuple-element.211), kind=kOutput, calls=%fused_computation.2.clone.1 | convolution fusion | flops 402653184 | bytes 1573376 | tf_op jit(solution)/shard_map/while/body/eval_jaxpr/dot_general | solution.py:25
  47.0 2.2 %fusion.70 = f32[512,128]{1,0:T(8,128)S(1)} fusion(f32[512,128]{1,0:T(8,128)S(1)} %copy.26, f32[11,512,512]{2,1,0:T(8,128)} %get-tuple-element.220, s32[]{:T(128)} %get-tuple-element.211), kind=kOutput, calls=%fused_computation.2.clone.1 | convolution fusion | flops 402653184 | bytes 1573376 | tf_op jit(solution)/shard_map/while/body/eval_jaxpr/dot_general | solution.py:25
  51.5 2.2 %fusion.70 = f32[512,128]{1,0:T(8,128)S(1)} fusion(f32[512,128]{1,0:T(8,128)S(1)} %copy.26, f32[11,512,512]{2,1,0:T(8,128)} %get-tuple-element.220, s32[]{:T(128)} %get-tuple-element.211), kind=kOutput, calls=%fused_computation.2.clone.1 | convolution fusion | flops 402653184 | bytes 1573376 | tf_op jit(solution)/shard_map/while/body/eval_jaxpr/dot_general | solution.py:25
  56.0 2.2 %fusion.70 = f32[512,128]{1,0:T(8,128)S(1)} fusion(f32[512,128]{1,0:T(8,128)S(1)} %copy.26, f32[11,512,512]{2,1,0:T(8,128)} %get-tuple-element.220, s32[]{:T(128)} %get-tuple-element.211), kind=kOutput, calls=%fused_computation.2.clone.1 | convolution fusion | flops 402653184 | bytes 1573376 | tf_op jit(solution)/shard_map/while/body/eval_jaxpr/dot_general | solution.py:25
  60.5 2.2 %fusion.70 = f32[512,128]{1,0:T(8,128)S(1)} fusion(f32[512,128]{1,0:T(8,128)S(1)} %copy.26, f32[11,512,512]{2,1,0:T(8,128)} %get-tuple-element.220, s32[]{:T(128)} %get-tuple-element.211), kind=kOutput, calls=%fused_computation.2.clone.1 | convolution fusion | flops 402653184 | bytes 1573376 | tf_op jit(solution)/shard_map/while/body/eval_jaxpr/dot_general | solution.py:25
  65.0 2.2 %fusion.70 = f32[512,128]{1,0:T(8,128)S(1)} fusion(f32[512,128]{1,0:T(8,128)S(1)} %copy.26, f32[11,512,512]{2,1,0:T(8,128)} %get-tuple-element.220, s32[]{:T(128)} %get-tuple-element.211), kind=kOutput, calls=%fused_computation.2.clone.1 | convolution fusion | flops 402653184 | bytes 1573376 | tf_op jit(solution)/shard_map/while/body/eval_jaxpr/dot_general | solution.py:25
  67.9 5.2 %collective-permute-done = f32[512,128]{1,0:T(8,128)S(1)} collective-permute-done((f32[512,128]{1,0:T(8,128)S(1)}, f32[512,128]{1,0:T(8,128)S(1)}, u32[]{:S(2)}, u32[]{:S(2)}) %collective-permute-start) | collective-permute-done | bytes 262176 | tf_op jit(solution)/shard_map/ppermute | solution.py:12
  73.1 5.8 %collective-permute-done.1 = f32[512,128]{1,0:T(8,128)S(1)} collective-permute-done((f32[512,128]{1,0:T(8,128)S(1)}, f32[512,128]{1,0:T(8,128)S(1)}, u32[]{:S(2)}, u32[]{:S(2)}) %collective-permute-start.1) | collective-permute-done | bytes 262176 | tf_op jit(solution)/shard_map/ppermute | solution.py:12
  78.9 3.1 %collective-permute-start.3 = (f32[512,128]{1,0:T(8,128)S(1)}, f32[512,128]{1,0:T(8,128)S(1)}, u32[]{:S(2)}, u32[]{:S(2)}) collective-permute-start(f32[512,128]{1,0:T(8,128)S(1)} %get-tuple-element.108), channel_id=1, source_target_pairs={{0,4},{4,8},{8,12},{12,16},{16,20},{20,24},{24,28},{1,5},{5,9},{9,... | collective-permute-start | bytes 786440 | tf_op jit(solution)/shard_map/ppermute | solution.py:21
  82.2 2.5 %collective-permute-done.2 = f32[512,128]{1,0:T(8,128)S(1)} collective-permute-done((f32[512,128]{1,0:T(8,128)S(1)}, f32[512,128]{1,0:T(8,128)S(1)}, u32[]{:S(2)}, u32[]{:S(2)}) %collective-permute-start.2) | collective-permute-done | bytes 262176 | tf_op jit(solution)/shard_map/ppermute | solution.py:12
  85.3 2.7 %collective-permute-done.3 = f32[512,128]{1,0:T(8,128)S(1)} collective-permute-done((f32[512,128]{1,0:T(8,128)S(1)}, f32[512,128]{1,0:T(8,128)S(1)}, u32[]{:S(2)}, u32[]{:S(2)}) %collective-permute-start.3) | collective-permute-done | bytes 262176 | tf_op jit(solution)/shard_map/ppermute | solution.py:21
  89.2 2.5 %collective-permute-start.4 = (f32[512,128]{0,1:T(8,128)S(1)}, f32[512,128]{0,1:T(8,128)S(1)}, u32[]{:S(2)}, u32[]{:S(2)}) collective-permute-start(f32[512,128]{0,1:T(8,128)S(1)} %convolution_select_fusion.2), channel_id=1, source_target_pairs={{0,3},{1,0},{2,1},{3,2},{4,7},{5,4},{6,5},{7,6},{8,11},{9,8},{10,9... | collective-permute-start | bytes 786440 | tf_op jit(solution)/shard_map/ppermute | solution.py:12
  91.7 5.1 %collective-permute-done.4 = f32[512,128]{0,1:T(8,128)S(1)} collective-permute-done((f32[512,128]{0,1:T(8,128)S(1)}, f32[512,128]{0,1:T(8,128)S(1)}, u32[]{:S(2)}, u32[]{:S(2)}) %collective-permute-start.4) | collective-permute-done | bytes 262176 | tf_op jit(solution)/shard_map/ppermute | solution.py:12
  96.8 5.8 %collective-permute-done.5 = f32[512,128]{0,1:T(8,128)S(1)} collective-permute-done((f32[512,128]{0,1:T(8,128)S(1)}, f32[512,128]{0,1:T(8,128)S(1)}, u32[]{:S(2)}, u32[]{:S(2)}) %collective-permute-start.5) | collective-permute-done | bytes 262176 | tf_op jit(solution)/shard_map/ppermute | solution.py:12
  103.9 4.8 %collective-permute-done.6 = f32[512,128]{0,1:T(8,128)S(1)} collective-permute-done((f32[512,128]{0,1:T(8,128)S(1)}, f32[512,128]{0,1:T(8,128)S(1)}, u32[]{:S(2)}, u32[]{:S(2)}) %collective-permute-start.6) | collective-permute-done | bytes 262176 | tf_op jit(solution)/shard_map/ppermute | solution.py:12
  114.0 2.2 %collective-permute-start.12 = (f32[512]{0:T(512)S(1)}, f32[512]{0:T(512)S(1)}, u32[]{:S(2)}, u32[]{:S(2)}) collective-permute-start(f32[512]{0:T(512)S(1)} %get-tuple-element.109), channel_id=1, source_target_pairs={{0,4},{4,8},{8,12},{12,16},{16,20},{20,24},{24,28},{1,5},{5,9},{9,... | collective-permute-start | bytes 6152 | tf_op jit(solution)/shard_map/ppermute | solution.py:21
  127.4 2.8 %collective-permute-done.10 = f32[512,128]{0,1:T(8,128)S(1)} collective-permute-done((f32[512,128]{0,1:T(8,128)S(1)}, f32[512,128]{0,1:T(8,128)S(1)}, u32[]{:S(2)}, u32[]{:S(2)}) %collective-permute-start.10) | collective-permute-done | bytes 262176 | tf_op jit(solution)/shard_map/ppermute | solution.py:12
  131.7 6.2 %collective-permute-done.14 = f32[512]{0:T(512)S(1)} collective-permute-done((f32[512]{0:T(512)S(1)}, f32[512]{0:T(512)S(1)}, u32[]{:S(2)}, u32[]{:S(2)}) %collective-permute-start.14) | collective-permute-done | bytes 2080 | tf_op jit(solution)/shard_map/ppermute | solution.py:21
  139.6 7.0 %all-reduce = f32[512]{0:T(512)S(1)} all-reduce(f32[512]{0:T(512)S(1)} %bitcast.87), channel_id=2, replica_groups=mesh['tm'=8,'col'=4] {'col'}, use_global_device_ids=true, to_apply=%region_2.4.clone | all-reduce | flops 512 | bytes 4096
  148.6 3.3 %collective-permute-done.15 = f32[128]{0:T(128)S(1)} collective-permute-done((f32[128]{0:T(128)S(1)}, f32[128]{0:T(128)S(1)}, u32[]{:S(2)}, u32[]{:S(2)}) %collective-permute-start.15) | collective-permute-done | bytes 544 | tf_op jit(solution)/shard_map/ppermute | solution.py:21
  151.9 7.0 %all-gather = f32[4,1,128]{2,1,0:T(1,128)S(1)} all-gather(f32[1,1,128]{2,1,0:T(1,128)S(1)} %fusion.33), channel_id=1, replica_groups=mesh['tm'=8,'col'=4] {'col'}, dimensions={0}, use_global_device_ids=true | all-gather | bytes 2560 | tf_op jit(solution)/shard_map/all_gather | solution.py:65
  158.9 25.8 %while.27 = (s32[]{:T(128)}, f32[512]{0:T(512)S(1)}, f32[11,128]{1,0:T(8,128)S(1)}, f32[11,512,512]{2,1,0:T(8,128)}, f32[11,512]{1,0:T(8,128)S(1)}, /*index=5*/s32[]{:T(128)}, s32[]{:T(128)}, s32[]{:T(128)}) while((s32[]{:T(128)}, f32[512]{0:T(512)S(1)}, f32[11,128]{1,0:T(8,128)S(1)}, f32[11,512,512]{2,1,0:T(8,128)}, f32[11,512]{1,0:T(8,128)S(1)}, ...), condition=%wide.region_4.6_spmd, body=%wide.region_3.5_spmd.sunk | while | flops 3146242 | bytes 1065569 | solution.py:72
  (146 shorter events, 69.2 us)
Async XLA Ops:
  0.0 17.6 %copy-start = (f32[12,512]{1,0:T(8,128)S(1)}, f32[12,512]{1,0:T(8,128)}, u32[]{:S(2)}) copy-start(f32[12,512]{1,0:T(8,128)} %param.10) | copy-start | bytes 73732
  0.0 17.6 %slice-start = ((f32[12,512,512]{2,1,0:T(8,128)}), f32[1,512,512]{2,1,0:T(8,128)S(1)}, s32[]{:S(2)}) async-start(f32[12,512,512]{2,1,0:T(8,128)} %param.9), calls=%async_computation | async-start | bytes 2097152 | tf_op jit(solution)/shard_map/slice | solution.py:43
  0.0 17.7 %slice-start.1 = ((f32[12,512]{1,0:T(8,128)}), f32[1,512]{1,0:T(1,128)S(1)}, s32[]{:S(2)}) async-start(f32[12,512]{1,0:T(8,128)} %param.10), calls=%async_computation.1 | async-start | bytes 4096 | tf_op jit(solution)/shard_map/slice | solution.py:43
  67.2 5.9 %collective-permute-start = (f32[512,128]{1,0:T(8,128)S(1)}, f32[512,128]{1,0:T(8,128)S(1)}, u32[]{:S(2)}, u32[]{:S(2)}) collective-permute-start(f32[512,128]{1,0:T(8,128)S(1)} %get-tuple-element.108), channel_id=1, source_target_pairs={{0,3},{1,0},{2,1},{3,2},{4,7},{5,4},{6,5},{7,6},{8,11},{9,8},{10,9... | collective-permute-start | bytes 786440 | tf_op jit(solution)/shard_map/ppermute | solution.py:12
  73.1 5.8 %collective-permute-start.1 = (f32[512,128]{1,0:T(8,128)S(1)}, f32[512,128]{1,0:T(8,128)S(1)}, u32[]{:S(2)}, u32[]{:S(2)}) collective-permute-start(f32[512,128]{1,0:T(8,128)S(1)} %collective-permute-done), channel_id=1, source_target_pairs={{0,3},{1,0},{2,1},{3,2},{4,7},{5,4},{6,5},{7,6},{8,11},{9,8},{10,9... | collective-permute-start | bytes 786440 | tf_op jit(solution)/shard_map/ppermute | solution.py:12
  78.9 5.8 %collective-permute-start.2 = (f32[512,128]{1,0:T(8,128)S(1)}, f32[512,128]{1,0:T(8,128)S(1)}, u32[]{:S(2)}, u32[]{:S(2)}) collective-permute-start(f32[512,128]{1,0:T(8,128)S(1)} %collective-permute-done.1), channel_id=1, source_target_pairs={{0,3},{1,0},{2,1},{3,2},{4,7},{5,4},{6,5},{7,6},{8,11},{9,8},{10,9... | collective-permute-start | bytes 786440 | tf_op jit(solution)/shard_map/ppermute | solution.py:12
  78.9 9.1 %collective-permute-start.3 = (f32[512,128]{1,0:T(8,128)S(1)}, f32[512,128]{1,0:T(8,128)S(1)}, u32[]{:S(2)}, u32[]{:S(2)}) collective-permute-start(f32[512,128]{1,0:T(8,128)S(1)} %get-tuple-element.108), channel_id=1, source_target_pairs={{0,4},{4,8},{8,12},{12,16},{16,20},{20,24},{24,28},{1,5},{5,9},{9,... | collective-permute-start | bytes 786440 | tf_op jit(solution)/shard_map/ppermute | solution.py:21
  89.2 7.6 %collective-permute-start.4 = (f32[512,128]{0,1:T(8,128)S(1)}, f32[512,128]{0,1:T(8,128)S(1)}, u32[]{:S(2)}, u32[]{:S(2)}) collective-permute-start(f32[512,128]{0,1:T(8,128)S(1)} %convolution_select_fusion.2), channel_id=1, source_target_pairs={{0,3},{1,0},{2,1},{3,2},{4,7},{5,4},{6,5},{7,6},{8,11},{9,8},{10,9... | collective-permute-start | bytes 786440 | tf_op jit(solution)/shard_map/ppermute | solution.py:12
  96.8 5.8 %collective-permute-start.5 = (f32[512,128]{0,1:T(8,128)S(1)}, f32[512,128]{0,1:T(8,128)S(1)}, u32[]{:S(2)}, u32[]{:S(2)}) collective-permute-start(f32[512,128]{0,1:T(8,128)S(1)} %collective-permute-done.4), channel_id=1, source_target_pairs={{0,3},{1,0},{2,1},{3,2},{4,7},{5,4},{6,5},{7,6},{8,11},{9,8},{10,9... | collective-permute-start | bytes 786440 | tf_op jit(solution)/shard_map/ppermute | solution.py:12
  102.6 6.1 %collective-permute-start.6 = (f32[512,128]{0,1:T(8,128)S(1)}, f32[512,128]{0,1:T(8,128)S(1)}, u32[]{:S(2)}, u32[]{:S(2)}) collective-permute-start(f32[512,128]{0,1:T(8,128)S(1)} %collective-permute-done.5), channel_id=1, source_target_pairs={{0,3},{1,0},{2,1},{3,2},{4,7},{5,4},{6,5},{7,6},{8,11},{9,8},{10,9... | collective-permute-start | bytes 786440 | tf_op jit(solution)/shard_map/ppermute | solution.py:12
  102.6 9.0 %collective-permute-start.7 = (f32[512,128]{0,1:T(8,128)S(1)}, f32[512,128]{0,1:T(8,128)S(1)}, u32[]{:S(2)}, u32[]{:S(2)}) collective-permute-start(f32[512,128]{0,1:T(8,128)S(1)} %convolution_select_fusion.2), channel_id=1, source_target_pairs={{0,8},{4,12},{8,16},{12,20},{16,24},{20,28},{1,9},{5,13},{9,17},{1... | collective-permute-start | bytes 786440 | tf_op jit(solution)/shard_map/ppermute | solution.py:21
  103.9 17.6 %copy-start.2 = (u32[32]{0:T(128)S(1)}, u32[32]{0:T(128)}, u32[]{:S(2)}) copy-start(u32[32]{0:T(128)} %constant.75) | copy-start | bytes 388
  112.3 5.9 %collective-permute-start.8 = (f32[512,128]{0,1:T(8,128)S(1)}, f32[512,128]{0,1:T(8,128)S(1)}, u32[]{:S(2)}, u32[]{:S(2)}) collective-permute-start(f32[512,128]{0,1:T(8,128)S(1)} %convolution_select_fusion.1), channel_id=1, source_target_pairs={{0,3},{1,0},{2,1},{3,2},{4,7},{5,4},{6,5},{7,6},{8,11},{9,8},{10,9... | collective-permute-start | bytes 786440 | tf_op jit(solution)/shard_map/ppermute | solution.py:12
  114.0 5.2 %collective-permute-start.12 = (f32[512]{0:T(512)S(1)}, f32[512]{0:T(512)S(1)}, u32[]{:S(2)}, u32[]{:S(2)}) collective-permute-start(f32[512]{0:T(512)S(1)} %get-tuple-element.109), channel_id=1, source_target_pairs={{0,4},{4,8},{8,12},{12,16},{16,20},{20,24},{24,28},{1,5},{5,9},{9,... | collective-permute-start | bytes 6152 | tf_op jit(solution)/shard_map/ppermute | solution.py:21
  118.2 5.8 %collective-permute-start.9 = (f32[512,128]{0,1:T(8,128)S(1)}, f32[512,128]{0,1:T(8,128)S(1)}, u32[]{:S(2)}, u32[]{:S(2)}) collective-permute-start(f32[512,128]{0,1:T(8,128)S(1)} %collective-permute-done.8), channel_id=1, source_target_pairs={{0,3},{1,0},{2,1},{3,2},{4,7},{5,4},{6,5},{7,6},{8,11},{9,8},{10,9... | collective-permute-start | bytes 786440 | tf_op jit(solution)/shard_map/ppermute | solution.py:12
  120.2 5.1 %collective-permute-start.13 = (f32[512]{0:T(512)S(1)}, f32[512]{0:T(512)S(1)}, u32[]{:S(2)}, u32[]{:S(2)}) collective-permute-start(f32[512]{0:T(512)S(1)} %add_select_fusion.2), channel_id=1, source_target_pairs={{0,8},{4,12},{8,16},{12,20},{16,24},{20,28},{1,9},{5,13},{9,17},{1... | collective-permute-start | bytes 6152 | tf_op jit(solution)/shard_map/ppermute | solution.py:21
  122.7 15.8 %collective-permute-start.11 = (f32[512,128]{0,1:T(8,128)S(1)}, f32[512,128]{0,1:T(8,128)S(1)}, u32[]{:S(2)}, u32[]{:S(2)}) collective-permute-start(f32[512,128]{0,1:T(8,128)S(1)} %convolution_select_fusion.1), channel_id=1, source_target_pairs={{0,16},{4,20},{8,24},{12,28},{1,17},{5,21},{9,25},{13,29},{2,18},{... | collective-permute-start | bytes 786440 | tf_op jit(solution)/shard_map/ppermute | solution.py:21
  124.0 6.1 %collective-permute-start.10 = (f32[512,128]{0,1:T(8,128)S(1)}, f32[512,128]{0,1:T(8,128)S(1)}, u32[]{:S(2)}, u32[]{:S(2)}) collective-permute-start(f32[512,128]{0,1:T(8,128)S(1)} %collective-permute-done.9), channel_id=1, source_target_pairs={{0,3},{1,0},{2,1},{3,2},{4,7},{5,4},{6,5},{7,6},{8,11},{9,8},{10,9... | collective-permute-start | bytes 786440 | tf_op jit(solution)/shard_map/ppermute | solution.py:12
  125.9 13.4 %copy-start.1 = (f32[128]{0:T(128)S(1)}, f32[128]{0:T(128)}, u32[]{:S(2)}) copy-start(f32[128]{0:T(128)} %param.11) | copy-start | bytes 1540
  125.9 12.0 %collective-permute-start.14 = (f32[512]{0:T(512)S(1)}, f32[512]{0:T(512)S(1)}, u32[]{:S(2)}, u32[]{:S(2)}) collective-permute-start(f32[512]{0:T(512)S(1)} %add_select_fusion.1), channel_id=1, source_target_pairs={{0,16},{4,20},{8,24},{12,28},{1,17},{5,21},{9,25},{13,29},{2,18},{... | collective-permute-start | bytes 6152 | tf_op jit(solution)/shard_map/ppermute | solution.py:21
  146.7 5.2 %collective-permute-start.15 = (f32[128]{0:T(128)S(1)}, f32[128]{0:T(128)S(1)}, u32[]{:S(2)}, u32[]{:S(2)}) collective-permute-start(f32[128]{0:T(128)S(1)} %dynamic-slice_add_fusion), channel_id=1, source_target_pairs={{0,4},{4,8},{8,12},{12,16},{16,20},{20,24},{24,28},{1,5},{5,9},{9,... | collective-permute-start | bytes 1544 | tf_op jit(solution)/shard_map/ppermute | solution.py:21
